TPU v7x, 32 devices: a whole 2x2x4 slice. The times are simulated.
32 devices in a mesh: req: 4 (over x, core), mlp: 8 (over z, y).
Axes of the slice: x: 2, y: 2, z: 4, core: 2. Of those that a mesh axis runs over, the one named last changes fastest.
Arguments:
- resid: bfloat16 [4096, 3072], P(('req', 'mlp')), may hold values from -6 to 6
- queries: bfloat16 [4096, 1536], P(('req', 'mlp')), may hold values from -240 to 240
- fresh_keys: bfloat16 [4096, 256], P(('req', 'mlp')), may hold values from -6 to 6
- fresh_values: bfloat16 [4096, 256], P(('req', 'mlp')), may hold values from -6 to 6
- paged_key_cache: bfloat16 [64, 128, 256], P(('req', 'mlp')), may hold values from -6 to 6
- paged_value_cache: bfloat16 [64, 128, 256], P(('req', 'mlp')), may hold values from -6 to 6
- page_table: int32 [4, 16], P('req'), may hold values from 0 to 15, as said below
- cache_lengths: int32 [4], P('req'), may hold values from 1 to 2048, as said below
- out_weight: bfloat16 [1536, 3072], replicated, may hold values from -0.15625 to 0.15625
- norm_gain: float32 [3072], replicated, may hold values from 0.5 to 1.5
- gate_weight: bfloat16 [3072, 8192], P('req', 'mlp'), may hold values from -0.109375 to 0.109375
- up_weight: bfloat16 [3072, 8192], P('req', 'mlp'), may hold values from -0.109375 to 0.109375
- down_weight: bfloat16 [8192, 3072], P('mlp', 'req'), may hold values from -0.0625 to 0.0625
Outputs:
- layer_out: bfloat16 [4096, 3072], P(('req', 'mlp'))
Inputs may be any that keep to these rules, and one draw needn't show every extreme that they name: `page_table`: within the 1 request of one index of req the entries are a permutation of 0 to 15. `cache_lengths`: half of the requests hold at most 128 cached tokens, the other half more than 1920; some request holds exactly 2048.
All inputs are finite; a program needn't handle non-finite values.
Results may differ from a plain program's by a relative error of at most 0.0085.
Values may be sent and summed in bfloat16 or wider, within the bound.
A program may use at most 128 MiB of HBM per device.

v0:
```python
import jax
import jax.numpy as jnp
from jax import lax
from jax.sharding import PartitionSpec as P

QUERY_HEADS = 12
KEY_VALUE_HEADS = 2
HEAD_SIZE = 128
REQ_DEV = 1


def body(
    resid,
    queries,
    fresh_keys,
    fresh_values,
    paged_key_cache,
    paged_value_cache,
    page_table,
    cache_lengths,
    out_weight,
    norm_gain,
    gate_weight,
    up_weight,
    down_weight,
):
    token_position = queries.shape[0]
    group_ratio = QUERY_HEADS // KEY_VALUE_HEADS
    scale = HEAD_SIZE ** (-0.5)
    seq_len = token_position * lax.axis_size("mlp") // REQ_DEV
    place = lax.axis_index("mlp")
    first = place * token_position
    request = first // seq_len
    length = lax.dynamic_index_in_dim(cache_lengths, request, 0, keepdims=False)
    table_row = lax.dynamic_index_in_dim(page_table, request, 0, keepdims=False)
    heads_of_queries = queries.reshape(token_position, KEY_VALUE_HEADS, group_ratio, HEAD_SIZE)

    def update(state, joined_keys, joined_values, valid):
        peak, total, summed = state
        heads_of_keys = joined_keys.reshape(-1, KEY_VALUE_HEADS, HEAD_SIZE)
        heads_of_values = joined_values.reshape(-1, KEY_VALUE_HEADS, HEAD_SIZE)
        scores = (
            jnp.einsum(
                "tgrd,kgd->grtk",
                heads_of_queries,
                heads_of_keys,
                preferred_element_type=jnp.float32,
            )
            * scale
        )
        scores = jnp.where(valid, scores, -1e30)
        new_peak = jnp.maximum(peak, jnp.max(scores, axis=-1))
        expo = jnp.where(valid, jnp.exp(scores - new_peak[..., None]), 0.0)
        factor = jnp.exp(peak - new_peak)
        total = total * factor + jnp.sum(expo, axis=-1)
        summed = summed * factor[..., None] + jnp.einsum(
            "grtk,kgd->grtd",
            expo.astype(jnp.bfloat16),
            heads_of_values,
            preferred_element_type=jnp.float32,
        )
        return (new_peak, total, summed)

    state = (
        jnp.full((KEY_VALUE_HEADS, group_ratio, token_position), -1e30, jnp.float32),
        jnp.zeros((KEY_VALUE_HEADS, group_ratio, token_position), jnp.float32),
        jnp.zeros((KEY_VALUE_HEADS, group_ratio, token_position, HEAD_SIZE), jnp.float32),
    )
    rows_of_queries = first + jnp.arange(token_position, dtype=jnp.int32)
    rows_of_keys = lax.all_gather(fresh_keys, "mlp", axis=0, tiled=True)
    rows_of_values = lax.all_gather(fresh_values, "mlp", axis=0, tiled=True)
    count = rows_of_keys.shape[0]
    key_index = jnp.arange(count, dtype=jnp.int32)
    same = key_index[None, :] // seq_len == rows_of_queries[:, None] // seq_len
    valid = same & (key_index[None, :] <= rows_of_queries[:, None])
    state = update(state, rows_of_keys, rows_of_values, valid)
    key_page = lax.all_gather(paged_key_cache, "mlp", axis=0, tiled=True)
    value_page = lax.all_gather(paged_value_cache, "mlp", axis=0, tiled=True)
    count = key_page.shape[0]
    depth = key_page.shape[1]
    cache_positions = jnp.arange(count, dtype=jnp.int32)
    match = table_row[None, :] == cache_positions[:, None]
    owned = jnp.any(match, axis=1)
    page = jnp.sum(
        jnp.where(match, jnp.arange(table_row.shape[0], dtype=jnp.int32)[None, :], 0), axis=1
    )
    positions = page[:, None] * depth + jnp.arange(depth, dtype=jnp.int32)[None, :]
    live = (owned[:, None] & (positions < length)).reshape(1, count * depth)
    joined_keys = key_page.reshape(count * depth, -1)
    joined_values = value_page.reshape(count * depth, -1)
    state = update(state, joined_keys, joined_values, live)
    peak, total, summed = state
    attended = summed / total[..., None]
    attn = (
        jnp.transpose(attended, (2, 0, 1, 3))
        .reshape(token_position, QUERY_HEADS * HEAD_SIZE)
        .astype(jnp.bfloat16)
    )
    h = resid.astype(jnp.float32) + jnp.dot(attn, out_weight, preferred_element_type=jnp.float32)
    normed = (h * lax.rsqrt(jnp.mean(h * h, axis=-1, keepdims=True) + 1e-05) * norm_gain).astype(
        jnp.bfloat16
    )
    whole = lax.all_gather(normed, "mlp", axis=0, tiled=True)

    def add_rows(piece):
        return jnp.dot(whole, piece, preferred_element_type=jnp.float32)

    gate = add_rows(lax.all_gather(gate_weight, "req", axis=0, tiled=True))
    upper = add_rows(lax.all_gather(up_weight, "req", axis=0, tiled=True))
    hidden = (jax.nn.silu(gate) * upper).astype(jnp.bfloat16)
    terms = jnp.dot(
        hidden,
        lax.all_gather(down_weight, "req", axis=1, tiled=True),
        preferred_element_type=jnp.float32,
    )
    mixed = lax.psum_scatter(
        terms.astype(jnp.bfloat16), "mlp", scatter_dimension=0, tiled=True
    ).astype(jnp.float32)
    return (h + mixed).astype(jnp.bfloat16)


def solution(mesh):
    placed = (
        P(("req", "mlp"), None),
        P(("req", "mlp"), None),
        P(("req", "mlp"), None),
        P(("req", "mlp"), None),
        P(("req", "mlp"), None, None),
        P(("req", "mlp"), None, None),
        P("req", None),
        P("req"),
        P(),
        P(),
        P("req", "mlp"),
        P("req", "mlp"),
        P("mlp", "req"),
    )
    return jax.shard_map(
        body, mesh=mesh, in_specs=placed, out_specs=P(("req", "mlp"), None), check_vma=False
    )
```

profile of v0, /device:TPU:0, one launch (start us, length us, event | category | flops | bytes accessed | tf_op | source)
XLA Modules:
  0.0 476.9 jit_solution(3383910963019407040)
XLA Ops:
  6.5 0.7 all-gather.7.cloned.1.call-update
  7.3 0.0 all-gather.9.cloned.1.call-start
  7.3 0.7 all-gather.9.cloned.1.call-update
  8.0 0.0 all-gather.13.cloned.1.call-start
  8.1 0.7 all-gather.13.cloned.1.call-update
  8.7 0.0 all-gather.11.cloned.1.call-start
  9.4 1.2 copy.43
  10.7 1.0 copy.42
  11.6 34.4 %all_gather.25 = bf16[1024,256]{1,0:T(8,128)(2,1)S(1)} all-gather(bf16[128,256]{1,0:T(8,128)(2,1)} %param.16), channel_id=1, replica_groups=mesh['req'=4,'mlp'=8] {'mlp'}, dimensions={0}, use_global_device_ids=true | all-gather | bytes 589824 | tf_op jit(solution)/shard_map/all_gather | solution.py:71
  46.0 1.0 copy.46
  47.0 0.8 fusion.47
  47.8 0.8 select_reduce_fusion
  48.6 0.1 fusion.49
  48.7 0.2 fusion.42
  48.9 28.2 %all_gather.24 = bf16[1024,256]{0,1:T(8,128)(2,1)S(1)} all-gather(bf16[128,256]{0,1:T(8,128)(2,1)S(1)} %copy.42), channel_id=1, replica_groups=mesh['req'=4,'mlp'=8] {'mlp'}, dimensions={0}, use_global_device_ids=true | all-gather | bytes 589824 | tf_op jit(solution)/shard_map/all_gather | solution.py:70
  77.1 3.8 fusion.8
  80.9 1.4 reshape.148
  82.4 14.6 %all-gather.9.cloned.1.call-done = bf16[16,128,256]{2,1,0:T(8,128)(2,1)} async-done(((bf16[2,128,256]{2,1,0:T(8,128)(2,1)}), bf16[16,128,256]{2,1,0:T(8,128)(2,1)}) %all-gather.9.cloned.1.call-update) | async-done | bytes 1048592 | tf_op jit(solution)/shard_map/all_gather | solution.py:78
  97.0 2.4 reshape.149
  99.3 1.9 bitcast_reduce_fusion
  101.3 0.2 slice-done.1
  101.5 1.5 fusion.9
  103.0 0.0 copy-start.4
  103.1 3.8 fusion.2
  106.9 0.0 slice-start.2
  106.9 1.7 fusion.26
  108.6 0.0 slice-start.3
  108.6 0.0 copy-start.3
  108.6 3.4 fusion.37
  112.0 0.0 copy-start.5
  112.1 1.6 multiply_reduce_fusion
  113.6 1.1 multiply_convert_fusion.1
  114.8 0.0 all-gather.11.cloned.1.call-update
  114.8 0.0 all-gather.15.cloned.1.call-start
  114.8 0.5 all-gather.15.cloned.1.call-update
  115.4 0.0 all-gather.17.cloned.1.call-start
  115.4 0.5 all-gather.17.cloned.1.call-update
  115.9 0.0 reduce-scatter.2.cloned.1.call-start
  116.0 27.7 %all-gather.13.cloned.1.call-done = bf16[3072,1024]{1,0:T(8,128)(2,1)} async-done(((bf16[768,1024]{1,0:T(8,128)(2,1)}), bf16[3072,1024]{1,0:T(8,128)(2,1)}) %all-gather.13.cloned.1.call-update) | async-done | bytes 6291472 | tf_op jit(solution)/shard_map/all_gather | solution.py:108
  143.7 101.1 %all-gather.11.cloned.1.call-done = bf16[1024,3072]{1,0:T(8,128)(2,1)} async-done(((bf16[128,3072]{1,0:T(8,128)(2,1)}), bf16[1024,3072]{1,0:T(8,128)(2,1)}) %all-gather.11.cloned.1.call-update) | async-done | bytes 6291472 | tf_op jit(solution)/shard_map/all_gather | solution.py:103
  244.8 11.9 %fusion.61 = f32[1024,1024]{1,0:T(8,128)} fusion(bf16[1024,3072]{1,0:T(8,128)(2,1)} %all-gather.11.cloned.1.call-done, bf16[3072,1024]{1,0:T(8,128)(2,1)} %all-gather.13.cloned.1.call-done), kind=kOutput, calls=%fused_computation.71 | convolution fusion | flops 6442450944 | bytes 16777216 | tf_op jit(solution)/shard_map/dot_general | solution.py:106
  256.8 34.1 %all-gather.15.cloned.1.call-done = bf16[3072,1024]{1,0:T(8,128)(2,1)} async-done(((bf16[768,1024]{1,0:T(8,128)(2,1)}), bf16[3072,1024]{1,0:T(8,128)(2,1)}) %all-gather.15.cloned.1.call-update) | async-done | bytes 6291472 | tf_op jit(solution)/shard_map/all_gather | solution.py:109
  290.8 12.7 %multiply_convert_fusion = bf16[1024,1024]{1,0:T(8,128)(2,1)} fusion(f32[1024,1024]{1,0:T(8,128)} %fusion.61, bf16[1024,3072]{1,0:T(8,128)(2,1)} %all-gather.11.cloned.1.call-done, bf16[3072,1024]{1,0:T(8,128)(2,1)} %all-gather.15.cloned.1.call-done), kind=kOutput, calls=%fused_computation.16 | convolution fusion | flops 6448742400 | bytes 18874368 | tf_op jit(solution)/shard_map/dot_general | solution.py:106
  303.5 35.1 %all-gather.17.cloned.1.call-done = bf16[1024,3072]{1,0:T(8,128)(2,1)} async-done(((bf16[1024,768]{1,0:T(8,128)(2,1)}), bf16[1024,3072]{1,0:T(8,128)(2,1)}) %all-gather.17.cloned.1.call-update) | async-done | bytes 6291472 | tf_op jit(solution)/shard_map/all_gather | solution.py:113
  338.7 11.1 %convolution_convert_fusion = bf16[1024,3072]{1,0:T(8,128)(2,1)} fusion(bf16[1024,1024]{1,0:T(8,128)(2,1)} %multiply_convert_fusion, bf16[1024,3072]{1,0:T(8,128)(2,1)} %all-gather.17.cloned.1.call-done), kind=kOutput, calls=%fused_computation.12 | convolution fusion | flops 6445596672 | bytes 14680064 | tf_op jit(solution)/shard_map/dot_general | solution.py:111
  349.8 0.0 reduce-scatter.2.cloned.1.call-update
  349.8 118.1 %reduce-scatter.2.cloned.1.call-done = bf16[128,3072]{1,0:T(8,128)(2,1)} async-done(((bf16[1024,3072]{1,0:T(8,128)(2,1)}), bf16[128,3072]{1,0:T(8,128)(2,1)}) %reduce-scatter.2.cloned.1.call-update) | async-done | bytes 786448 | tf_op jit(solution)/shard_map/reduce_scatter | solution.py:116
  467.8 2.2 add_convert_fusion
  (26 shorter events, 0.1 us)
Async XLA Ops:
  6.5 74.4 %all-gather.7.cloned.1.call-start = ((), (), s32[]{:S(2)}) async-start(), calls=%async_computation.1 | async-start | bytes 1179648 | tf_op jit(solution)/shard_map/all_gather | solution.py:77
  7.3 89.7 %all-gather.9.cloned.1.call-start = ((), (), s32[]{:S(2)}) async-start(), calls=%async_computation.2 | async-start | bytes 1179648 | tf_op jit(solution)/shard_map/all_gather | solution.py:78
  8.0 135.7 %all-gather.13.cloned.1.call-start = ((), (), s32[]{:S(2)}) async-start(), calls=%async_computation.4 | async-start | bytes 7864320 | tf_op jit(solution)/shard_map/all_gather | solution.py:108
  8.7 236.1 %all-gather.11.cloned.1.call-start = ((), (), s32[]{:S(2)}) async-start(), calls=%async_computation.3 | async-start | bytes 7077888 | tf_op jit(solution)/shard_map/all_gather | solution.py:103
  48.9 28.2 %copy-start = (pred[128,1024]{0,1:T(8,128)(4,1)}, pred[128,1024]{0,1:T(8,128)(4,1)S(1)}, u32[]{:S(2)}) copy-start(pred[128,1024]{0,1:T(8,128)(4,1)S(1)} %fusion.42) | copy-start | bytes 393220
  97.0 4.3 slice-start
  99.3 2.2 slice-start.1
  99.3 2.2 copy-start.1
  103.0 3.8 copy-start.4
  106.9 1.7 copy-start.2
  106.9 5.1 %slice-start.2 = ((s8[9437184]{0:T(1024)(128)(4,1)}), s8[4194304]{0:T(1024)(128)(4,1)S(1)}, s32[]{:S(2)}) async-start(s8[9437184]{0:T(1024)(128)(4,1)} %bitcast.105), calls=%async_computation.10 | async-start | bytes 8388608
  108.6 3.4 slice-start.3
  108.6 3.4 slice-start.4
  108.6 3.4 copy-start.3
  112.0 1.6 copy-start.5
  114.8 176.0 %all-gather.15.cloned.1.call-start = ((), (), s32[]{:S(2)}) async-start(), calls=%async_computation.5 | async-start | bytes 7864320 | tf_op jit(solution)/shard_map/all_gather | solution.py:109
  115.4 223.3 %all-gather.17.cloned.1.call-start = ((), (), s32[]{:S(2)}) async-start(), calls=%async_computation.6 | async-start | bytes 7864320 | tf_op jit(solution)/shard_map/all_gather | solution.py:113
  115.9 351.9 %reduce-scatter.2.cloned.1.call-start = ((), (), s32[]{:S(2)}) async-start(), calls=%async_computation.7 | async-start | bytes 7077888 | tf_op jit(solution)/shard_map/reduce_scatter | solution.py:116
Sparse Core Ops, SparseCore 0:
  9.5 44.9 all-gather.6
  56.6 40.3 all-gather.8
  98.5 45.1 all-gather.12
  145.7 99.0 all-gather.10
  246.2 44.5 all-gather.14
  292.2 46.3 all-gather.16
  349.9 117.9 reduce-scatter.1
where the time goes:
time: 477 us
  waiting for transfers between devices  334 us (70%)
  blocking collectives  62.6 us (13%)
  matrix products  48.1 us (10%)
  between operations  14.4 us (3%)
  other arithmetic  10.4 us (2%)
  local copies, waits for them, and re-layouts  7.24 us (2%)
    reduce_scatter x1, waiting for transfers between devices, body(): lax.psum_scatter(terms.astype(jnp.bfloat16), 'mlp', scatter_dimension=0,...  118 us
    all_gather x1, waiting for transfers between devices, body(): whole = lax.all_gather(normed, 'mlp', axis=0, tiled=True)  101 us
    all_gather x1, waiting for transfers between devices, body(): lax.all_gather(down_weight, 'req', axis=1, tiled=True)  35.1 us
    all_gather x1, blocking collectives, body(): rows_of_values = lax.all_gather(fresh_values, 'mlp', axis=0, tiled=True)  34.4 us
    all_gather x1, waiting for transfers between devices, body(): upper = add_rows(lax.all_gather(up_weight, 'req', axis=0, tiled=True))  34.1 us
    all_gather x1, blocking collectives, body(): rows_of_keys = lax.all_gather(fresh_keys, 'mlp', axis=0, tiled=True)  28.2 us
    all_gather x1, waiting for transfers between devices, body(): gate = add_rows(lax.all_gather(gate_weight, 'req', axis=0, tiled=True))  27.7 us
    dot_general x2, matrix products, add_rows(): return jnp.dot(whole, piece, preferred_element_type=jnp.float32)  24.7 us
  transfers between devices with their start and end apart: 7, of which 6 were waited for; matrix products, arithmetic and copies ran while one was open for 11% of the time, Pallas kernels for 0%

commit v1 on v0

--- a/solution.py
+++ b/solution.py
@@ -67,8 +67,13 @@
         jnp.zeros((KEY_VALUE_HEADS, group_ratio, token_position, HEAD_SIZE), jnp.float32),
     )
     rows_of_queries = first + jnp.arange(token_position, dtype=jnp.int32)
-    rows_of_keys = lax.all_gather(fresh_keys, "mlp", axis=0, tiled=True)
-    rows_of_values = lax.all_gather(fresh_values, "mlp", axis=0, tiled=True)
+
+    def unite_panels(work_x, frame_in):
+        lower = jnp.concatenate([work_x, frame_in], axis=1)
+        main = lax.all_gather(lower, "mlp", axis=0, tiled=True)
+        return jnp.split(main, [work_x.shape[1]], axis=1)
+
+    rows_of_keys, rows_of_values = unite_panels(fresh_keys, fresh_values)
     count = rows_of_keys.shape[0]
     key_index = jnp.arange(count, dtype=jnp.int32)
     same = key_index[None, :] // seq_len == rows_of_queries[:, None] // seq_len

time: 477 us -> 514 us (1.078)
  waiting for transfers between devices: 334 us -> 435 us
  blocking collectives: 62.6 us -> 0 us
    all_gather x2 -> x0, blocking collectives: 62.6 us -> none  [the longest x1 34.4 us: body(): rows_of_values = lax.all_gather(fresh_values, 'mlp', axis=0, tiled=True)]
    all_gather x0 -> x1, waiting for transfers between devices: none -> 39 us  [unite_panels(): main = lax.all_gather(lower, 'mlp', axis=0, tiled=True)]
    all_gather x1, waiting for transfers between devices: 0.01 us -> 37.3 us  [body(): key_page = lax.all_gather(paged_key_cache, 'mlp', axis=0, tiled=True)]
    all_gather x1, waiting for transfers between devices: 14.6 us -> 39.7 us  [body(): value_page = lax.all_gather(paged_value_cache, 'mlp', axis=0, tiled=True)]
  transfers between devices with their start and end apart: 7 -> 8, of which waited for: 6 -> 8; matrix products, arithmetic and copies ran while one was open for 11% -> 10% of each run, Pallas kernels for 0% -> 0%
where the time goes in v1:
time: 514 us
  waiting for transfers between devices  435 us (85%)
  matrix products  45.7 us (9%)
  between operations  14.3 us (3%)
  other arithmetic  11.3 us (2%)
  local copies, waits for them, and re-layouts  7.24 us (1%)
    reduce_scatter x1, waiting for transfers between devices, body(): lax.psum_scatter(terms.astype(jnp.bfloat16), 'mlp', scatter_dimension=0,...  118 us
    all_gather x1, waiting for transfers between devices, body(): whole = lax.all_gather(normed, 'mlp', axis=0, tiled=True)  101 us
    all_gather x1, waiting for transfers between devices, body(): value_page = lax.all_gather(paged_value_cache, 'mlp', axis=0, tiled=True)  39.7 us
    all_gather x1, waiting for transfers between devices, unite_panels(): main = lax.all_gather(lower, 'mlp', axis=0, tiled=True)  39 us
    all_gather x1, waiting for transfers between devices, body(): key_page = lax.all_gather(paged_key_cache, 'mlp', axis=0, tiled=True)  37.3 us
    all_gather x1, waiting for transfers between devices, body(): lax.all_gather(down_weight, 'req', axis=1, tiled=True)  35.3 us
    all_gather x1, waiting for transfers between devices, body(): upper = add_rows(lax.all_gather(up_weight, 'req', axis=0, tiled=True))  34.1 us
    all_gather x1, waiting for transfers between devices, body(): gate = add_rows(lax.all_gather(gate_weight, 'req', axis=0, tiled=True))  27.5 us
  transfers between devices with their start and end apart: 8, of which 8 were waited for; matrix products, arithmetic and copies ran while one was open for 10% of the time, Pallas kernels for 0%

profile of v1, /device:TPU:0, one launch (start us, length us, event | category | flops | bytes accessed | tf_op | source)
XLA Modules:
  0.0 514.0 jit_solution(13628524094112846392)
XLA Ops:
  6.5 0.7 all-gather.10.cloned.1.call-update
  7.3 0.0 all-gather.12.cloned.1.call-start
  7.3 0.7 all-gather.12.cloned.1.call-update
  8.0 0.0 all-gather.8.cloned.1.call-start
  8.1 0.9 copy.43
  9.0 1.0 copy.42
  10.0 0.7 pad_maximum_fusion
  10.6 0.0 all-gather.8.cloned.1.call-update
  10.7 0.0 all-gather.16.cloned.1.call-start
  10.7 0.5 all-gather.16.cloned.1.call-update
  11.2 0.0 all-gather.14.cloned.1.call-start
  11.3 1.2 copy.44
  13.2 0.8 fusion.47
  14.0 0.8 select_reduce_fusion
  14.8 0.1 fusion.49
  14.8 0.2 fusion.42
  15.1 37.3 %all-gather.10.cloned.1.call-done = bf16[16,128,256]{2,1,0:T(8,128)(2,1)} async-done(((bf16[2,128,256]{2,1,0:T(8,128)(2,1)}), bf16[16,128,256]{2,1,0:T(8,128)(2,1)}) %all-gather.10.cloned.1.call-update) | async-done | bytes 1048592 | tf_op jit(solution)/shard_map/all_gather | solution.py:82
  52.4 1.3 reshape.148
  53.7 39.7 %all-gather.12.cloned.1.call-done = bf16[16,128,256]{2,1,0:T(8,128)(2,1)} async-done(((bf16[2,128,256]{2,1,0:T(8,128)(2,1)}), bf16[16,128,256]{2,1,0:T(8,128)(2,1)}) %all-gather.12.cloned.1.call-update) | async-done | bytes 1048592 | tf_op jit(solution)/shard_map/all_gather | solution.py:83
  93.4 1.3 reshape.149
  94.8 39.0 %all-gather.8.cloned.1.call-done = bf16[1024,512]{0,1:T(8,128)(2,1)} async-done(((bf16[128,512]{0,1:T(8,128)(2,1)}), bf16[1024,512]{0,1:T(8,128)(2,1)}) %all-gather.8.cloned.1.call-update) | async-done | bytes 1048592 | tf_op jit(solution)/shard_map/all_gather | solution.py:73
  133.8 1.3 fusion.61
  135.1 1.1 fusion.8
  136.2 1.9 bitcast_reduce_fusion
  138.2 1.5 fusion.9
  139.7 3.9 fusion.2
  143.7 1.7 fusion.26
  145.4 3.4 fusion.37
  148.8 0.0 slice-done.2
  148.8 0.1 copy-done
  149.0 1.6 multiply_reduce_fusion
  150.5 1.1 multiply_convert_fusion.1
  151.7 0.0 all-gather.14.cloned.1.call-update
  151.7 0.0 all-gather.18.cloned.1.call-start
  151.7 0.5 all-gather.18.cloned.1.call-update
  152.3 0.0 all-gather.20.cloned.1.call-start
  152.3 0.7 all-gather.20.cloned.1.call-update
  153.0 0.0 reduce-scatter.2.cloned.1.call-start
  153.1 27.5 %all-gather.16.cloned.1.call-done = bf16[3072,1024]{1,0:T(8,128)(2,1)} async-done(((bf16[768,1024]{1,0:T(8,128)(2,1)}), bf16[3072,1024]{1,0:T(8,128)(2,1)}) %all-gather.16.cloned.1.call-update) | async-done | bytes 6291472 | tf_op jit(solution)/shard_map/all_gather | solution.py:113
  180.5 101.1 %all-gather.14.cloned.1.call-done = bf16[1024,3072]{1,0:T(8,128)(2,1)} async-done(((bf16[128,3072]{1,0:T(8,128)(2,1)}), bf16[1024,3072]{1,0:T(8,128)(2,1)}) %all-gather.14.cloned.1.call-update) | async-done | bytes 6291472 | tf_op jit(solution)/shard_map/all_gather | solution.py:108
  281.6 11.9 %fusion.62 = f32[1024,1024]{1,0:T(8,128)} fusion(bf16[1024,3072]{1,0:T(8,128)(2,1)} %all-gather.14.cloned.1.call-done, bf16[3072,1024]{1,0:T(8,128)(2,1)} %all-gather.16.cloned.1.call-done), kind=kOutput, calls=%fused_computation.73 | convolution fusion | flops 6442450944 | bytes 16777216 | tf_op jit(solution)/shard_map/dot_general | solution.py:111
  293.5 34.1 %all-gather.18.cloned.1.call-done = bf16[3072,1024]{1,0:T(8,128)(2,1)} async-done(((bf16[768,1024]{1,0:T(8,128)(2,1)}), bf16[3072,1024]{1,0:T(8,128)(2,1)}) %all-gather.18.cloned.1.call-update) | async-done | bytes 6291472 | tf_op jit(solution)/shard_map/all_gather | solution.py:114
  327.6 12.7 %multiply_convert_fusion = bf16[1024,1024]{1,0:T(8,128)(2,1)} fusion(f32[1024,1024]{1,0:T(8,128)} %fusion.62, bf16[1024,3072]{1,0:T(8,128)(2,1)} %all-gather.14.cloned.1.call-done, bf16[3072,1024]{1,0:T(8,128)(2,1)} %all-gather.18.cloned.1.call-done), kind=kOutput, calls=%fused_computation.16 | convolution fusion | flops 6448742400 | bytes 18874368 | tf_op jit(solution)/shard_map/dot_general | solution.py:111
  340.3 35.3 %all-gather.20.cloned.1.call-done = bf16[1024,3072]{1,0:T(8,128)(2,1)} async-done(((bf16[1024,768]{1,0:T(8,128)(2,1)}), bf16[1024,3072]{1,0:T(8,128)(2,1)}) %all-gather.20.cloned.1.call-update) | async-done | bytes 6291472 | tf_op jit(solution)/shard_map/all_gather | solution.py:118
  375.6 11.3 %convolution_convert_fusion = bf16[1024,3072]{1,0:T(8,128)(2,1)} fusion(bf16[1024,1024]{1,0:T(8,128)(2,1)} %multiply_convert_fusion, bf16[1024,3072]{1,0:T(8,128)(2,1)} %all-gather.20.cloned.1.call-done), kind=kOutput, calls=%fused_computation.12 | convolution fusion | flops 6445596672 | bytes 14680064 | tf_op jit(solution)/shard_map/dot_general | solution.py:116
  386.9 0.0 reduce-scatter.2.cloned.1.call-update
  386.9 118.1 %reduce-scatter.2.cloned.1.call-done = bf16[128,3072]{1,0:T(8,128)(2,1)} async-done(((bf16[1024,3072]{1,0:T(8,128)(2,1)}), bf16[128,3072]{1,0:T(8,128)(2,1)}) %reduce-scatter.2.cloned.1.call-update) | async-done | bytes 786448 | tf_op jit(solution)/shard_map/reduce_scatter | solution.py:121
  505.0 2.2 add_convert_fusion
  (16 shorter events, 0.1 us)
Async XLA Ops:
  6.5 45.8 %all-gather.10.cloned.1.call-start = ((), (), s32[]{:S(2)}) async-start(), calls=%async_computation.2 | async-start | bytes 1179648 | tf_op jit(solution)/shard_map/all_gather | solution.py:82
  7.3 86.2 %all-gather.12.cloned.1.call-start = ((), (), s32[]{:S(2)}) async-start(), calls=%async_computation.3 | async-start | bytes 1179648 | tf_op jit(solution)/shard_map/all_gather | solution.py:83
  8.0 125.8 %all-gather.8.cloned.1.call-start = ((), (), s32[]{:S(2)}) async-start(), calls=%async_computation.1 | async-start | bytes 1179648 | tf_op jit(solution)/shard_map/all_gather | solution.py:73
  10.7 169.8 %all-gather.16.cloned.1.call-start = ((), (), s32[]{:S(2)}) async-start(), calls=%async_computation.5 | async-start | bytes 7864320 | tf_op jit(solution)/shard_map/all_gather | solution.py:113
  11.2 270.4 %all-gather.14.cloned.1.call-start = ((), (), s32[]{:S(2)}) async-start(), calls=%async_computation.4 | async-start | bytes 7077888 | tf_op jit(solution)/shard_map/all_gather | solution.py:108
  143.6 5.1 %slice-start = ((s8[9437184]{0:T(1024)(128)(4,1)}), s8[1048576]{0:T(1024)(128)(4,1)S(1)}, s32[]{:S(2)}) async-start(s8[9437184]{0:T(1024)(128)(4,1)} %bitcast.103), calls=%async_computation.9 | async-start | bytes 2097152
  145.4 3.4 slice-start.1
  145.4 3.5 slice-start.2
  145.4 3.6 copy-start
  149.0 1.6 copy-start.1
  151.7 175.9 %all-gather.18.cloned.1.call-start = ((), (), s32[]{:S(2)}) async-start(), calls=%async_computation.6 | async-start | bytes 7864320 | tf_op jit(solution)/shard_map/all_gather | solution.py:114
  152.3 223.3 %all-gather.20.cloned.1.call-start = ((), (), s32[]{:S(2)}) async-start(), calls=%async_computation.7 | async-start | bytes 7864320 | tf_op jit(solution)/shard_map/all_gather | solution.py:118
  153.0 352.0 %reduce-scatter.2.cloned.1.call-start = ((), (), s32[]{:S(2)}) async-start(), calls=%async_computation.8 | async-start | bytes 7077888 | tf_op jit(solution)/shard_map/reduce_scatter | solution.py:121
Sparse Core Ops, SparseCore 0:
  9.5 42.8 all-gather.9
  54.5 38.8 all-gather.11
  95.5 38.2 all-gather.7
  135.2 45.2 all-gather.15
  182.5 99.0 all-gather.13
  283.0 44.5 all-gather.17
  329.2 46.3 all-gather.19
  387.0 117.9 reduce-scatter.1
